TPU v7x, 32 devices: a whole 2x2x4 slice. The times are simulated.
32 devices in a mesh: seq: 16 (over z, y, x), head: 2 (over core).
Axes of the slice: x: 2, y: 2, z: 4, core: 2. Of those that a mesh axis runs over, the one named last changes fastest.
Arguments:
- queries: float32 [8192, 4096], P('seq', 'head'), may hold values from -6 to 6
- keys: float32 [8192, 4096], P('seq', 'head'), may hold values from -6 to 6
- values: float32 [8192, 4096], P('seq', 'head'), may hold values from -6 to 6
- log_decay: float32 [32, 8192], P('head', 'seq'), may hold values from -1 to 0, as said below
- level_weights: float32 [32, 14, 8192], P('head', None, 'seq'), may hold values from 0.25 to 2.5
- norm_gain: float32 [4096], P('head'), may hold values from 0.1 to 1.9
- out_weight: float32 [4096, 2048], P('head', 'seq'), may hold values from -0.09375 to 0.09375
Outputs:
- mixed: float32 [8192, 2048], P('seq', 'head')
Inputs may be any that keep to these rules, and one draw needn't show every extreme that they name: `log_decay`: every entry is non-positive.
All inputs are finite; a program needn't handle non-finite values.
Results may differ from a plain program's by a relative error of at most 0.0003.
Values sent between devices are 32-bit elements; how exact they have to be, the bound alone decides.
A program may use at most 192 MiB of HBM per device.

v0:
```python
import jax
import jax.numpy as jnp
from jax import lax
from jax.sharding import PartitionSpec as P

HIGH = lax.Precision.HIGHEST


def entering(array, axis, combine, identity):
    size, mine = (lax.axis_size(axis), lax.axis_index(axis))
    everything = lax.all_gather(array, axis)
    start = jnp.broadcast_to(jnp.asarray(identity, array.dtype), array.shape)

    def step(k, before):
        reached = k < mine
        new = combine(before, everything[k])
        return jnp.where(reached, new, before)

    return lax.fori_loop(0, size, step, start)


def from_partner(value, axis, bit):
    mask = 2**bit
    pairs = [(source, source ^ mask) for source in range(lax.axis_size(axis))]
    return lax.ppermute(value, axis, pairs)


def add_pair(earlier, later):
    return earlier + later


def local(queries, keys, values, log_decay, level_weights, norm_gain, out_weight):
    head_count, tok_count = log_decay.shape
    feature_count = queries.shape[1]
    head_size = feature_count // head_count
    tok_bits = tok_count.bit_length() - 1
    seq_bits = lax.axis_size("seq").bit_length() - 1
    seq_index = lax.axis_index("seq")
    query_heads = queries.reshape(tok_count, head_count, head_size) * head_size ** (-0.5)
    key_heads = keys.reshape(tok_count, head_count, head_size)
    value_heads = values.reshape(tok_count, head_count, head_size)
    decay_sum = jnp.cumsum(log_decay, axis=1)
    span_decay = decay_sum[:, -1]
    positions = jnp.arange(tok_count, dtype=jnp.int32)
    mixed_bits = positions[:, None] ^ positions[None, :]
    level_ids = jnp.zeros((tok_count, tok_count), jnp.int32)
    for level_bit in range(tok_bits):
        level_ids = level_ids + (mixed_bits >> level_bit > 0).astype(jnp.int32)
    onehot = (level_ids[None] == jnp.arange(tok_bits + 1, dtype=jnp.int32)[:, None, None]).astype(
        jnp.float32
    )
    near = jnp.einsum("hli,lij->hij", level_weights[:, : tok_bits + 1, :], onehot, precision=HIGH)
    causal = positions[:, None] >= positions[None, :]
    gap = jnp.where(causal[None], decay_sum[:, :, None] - decay_sum[:, None, :], -jnp.inf)
    scores = (
        jnp.einsum("ihd,jhd->hij", query_heads, key_heads, precision=HIGH) * near * jnp.exp(gap)
    )
    local_out = jnp.einsum("hij,jhd->ihd", scores, value_heads, precision=HIGH)
    fade_weight = jnp.exp(span_decay[:, None] - decay_sum)
    own_state = jnp.einsum("jhd,hj,jhe->hde", key_heads, fade_weight, value_heads, precision=HIGH)
    level_states = []
    start_decay = entering(span_decay, "seq", add_pair, jnp.zeros_like(span_decay))
    block_state = own_state
    block_end = start_decay + span_decay
    for level_bit in range(seq_bits):
        other_state, other_end = from_partner((block_state, block_end), "seq", level_bit)
        is_upper = seq_index >> level_bit & 1 == 1
        reach = jnp.exp(jnp.where(is_upper, start_decay - other_end, -jnp.inf))
        level_states.append(reach[:, None, None] * other_state)
        low_state = jnp.where(is_upper, other_state, block_state)
        high_state = jnp.where(is_upper, block_state, other_state)
        low_end = jnp.where(is_upper, other_end, block_end)
        high_end = jnp.where(is_upper, block_end, other_end)
        block_state = jnp.exp(high_end - low_end)[:, None, None] * low_state + high_state
        block_end = high_end
    stacked = jnp.stack(level_states, axis=1)
    far_weight = level_weights[:, tok_bits + 1 :, :] * jnp.exp(decay_sum)[:, None, :]
    weighted = query_heads[:, :, None, :] * far_weight.transpose(2, 0, 1)[:, :, :, None]
    far_out = jnp.einsum("ihld,hlde->ihe", weighted, stacked, precision=HIGH)
    total_out = local_out + far_out
    root_mean = jnp.sqrt(jnp.mean(total_out * total_out, axis=-1, keepdims=True) + 1e-06)
    normed = (total_out / root_mean).reshape(tok_count, feature_count) * norm_gain
    partials = jnp.dot(
        normed,
        lax.all_gather(out_weight, "seq", axis=1, tiled=True),
        precision=HIGH,
        preferred_element_type=jnp.float32,
    )
    return lax.psum_scatter(partials, "head", scatter_dimension=1, tiled=True)


def solution(mesh):
    return jax.shard_map(
        local,
        mesh=mesh,
        in_specs=(
            P("seq", "head"),
            P("seq", "head"),
            P("seq", "head"),
            P("head", "seq"),
            P("head", None, "seq"),
            P("head"),
            P("head", "seq"),
        ),
        out_specs=P("seq", "head"),
        check_vma=False,
    )
```

profile of v0, /device:TPU:0, one launch (start us, length us, event | category | flops | bytes accessed | tf_op | source)
XLA Modules:
  0.0 380.0 jit_solution(9199074532487668545)
XLA Ops:
  7.3 1.2 reduce-window.6
  8.7 5.4 %copy.37 = f32[512,2048]{0,1:T(8,128)} copy(f32[512,2048]{1,0:T(8,128)} %param.11) | data formatting | bytes 8388608 | tf_op jit(solution)/shard_map/reshape | solution.py:41
  15.0 7.8 %fusion.36 = f32[16,128,128]{1,2,0:T(8,128)S(1)} fusion(f32[512,16,128]{0,2,1:T(8,128)} %bitcast.74, f32[512,16]{0,1:T(8,128)S(1)} %get-tuple-element.120, f32[512,2048]{1,0:T(8,128)} %param.10), kind=kOutput, calls=%fused_computation.41 | convolution fusion | flops 1611661312 | bytes 9469952 | tf_op jit(solution)/shard_map/jhd,hj,jhe->hde/dot_general | solution.py:60
  22.8 3.0 collective-permute-start.1
  27.4 64.2 %all-reduce = f32[256]{0:T(256)S(1)} all-reduce(f32[256]{0:T(256)S(1)} %dynamic-update-slice), channel_id=2, replica_groups=mesh['seq'=16,'head'=2] {'seq'}, use_global_device_ids=true, to_apply=%add | all-reduce | flops 256 | bytes 2048
  92.3 3.5 collective-permute-done
  95.9 3.6 collective-permute-done.2
  99.5 1.3 multiply_bitcast_fusion.4
  100.8 3.8 %copy.29 = f32[16,10,512]{1,0,2:T(8,128)} copy(f32[16,10,512]{2,0,1:T(8,128)S(1)} %slice-done) | data formatting | bytes 655360 | tf_op jit(solution)/shard_map/slice | solution.py:52
  104.7 1.2 convert_add_fusion
  105.8 19.2 %fusion.19 = f32[16,512,512]{2,1,0:T(8,128)} fusion(f32[512,2048]{1,0:T(8,128)} %param.9, f32[512,2048]{1,0:T(8,128)} %param.10), kind=kOutput, calls=%fused_computation.22 | convolution fusion | flops 6443499520 | bytes 25165824 | tf_op jit(solution)/shard_map/ihd,jhd->hij/dot_general | solution.py:56
  126.0 3.5 multiply_bitcast_fusion.3
  129.4 12.7 %fusion.9 = f32[512,512,16]{1,2,0:T(8,128)} fusion(f32[16,10,512]{1,0,2:T(8,128)S(1)} %copy-done.2, s32[512,512]{1,0:T(8,128)S(1)} %convert_add_fusion), kind=kOutput, calls=%fused_computation.12 | convolution fusion | flops 505937920 | bytes 18153472 | tf_op jit(solution)/shard_map/hli,lij->hij/dot_general | solution.py:52
  142.1 2.0 collective-permute-start.4
  144.1 49.7 %collective-permute-done.4 = f32[16]{0:T(128)S(1)} collective-permute-done((f32[16]{0:T(128)S(1)}, f32[16]{0:T(128)S(1)}, u32[]{:S(2)}, u32[]{:S(2)}) %collective-permute-start.4) | collective-permute-done | bytes 96 | tf_op jit(solution)/shard_map/ppermute | solution.py:25
  193.8 16.6 %collective-permute-done.6 = f32[16]{0:T(128)S(1)} collective-permute-done((f32[16]{0:T(128)S(1)}, f32[16]{0:T(128)S(1)}, u32[]{:S(2)}, u32[]{:S(2)}) %collective-permute-start.6) | collective-permute-done | bytes 96 | tf_op jit(solution)/shard_map/ppermute | solution.py:25
  210.5 1.7 multiply_bitcast_fusion.2
  212.2 38.5 %fusion.1 = f32[16,512,128]{1,2,0:T(8,128)} fusion(f32[512,16,128]{0,2,1:T(8,128)} %bitcast.75, f32[16,512,512]{2,1,0:T(8,128)} %fusion.19, f32[512,512,16]{1,2,0:T(8,128)} %fusion.9, f32[16,512]{1,0:T(8,128)S(1)} %copy_bitcast_fusion.1, pred[512,512]{1,0:T(8,128)(4,1)S(1)} %iota_compare_fusion.2), kind=kOutput, calls=%fused_computation.4 | convolution fusion | flops 6459228160 | bytes 42237952 | tf_op jit(solution)/shard_map/hij,jhd->ihd/dot_general | solution.py:58
  250.8 2.9 copy_bitcast_fusion
  253.7 51.6 %collective-permute-done.7 = f32[16,128,128]{1,2,0:T(8,128)S(1)} collective-permute-done((f32[16,128,128]{1,2,0:T(8,128)}, f32[16,128,128]{1,2,0:T(8,128)S(1)}, u32[]{:S(2)}, u32[]{:S(2)}) %collective-permute-start.7) | collective-permute-done | bytes 1048608 | tf_op jit(solution)/shard_map/ppermute | solution.py:25
  305.5 22.1 %multiply_reduce_fusion = (f32[512,16]{0,1:T(8,128)S(1)}, f32[512,16,128]{0,2,1:T(8,128)S(1)}) fusion(f32[512,16,4]{0,1,2:T(8,128)S(1)} %multiply_bitcast_fusion.5, f32[512,16,128]{2,0,1:T(8,128)S(1)} %copy_bitcast_fusion, f32[16,1,128,128]{2,3,0,1:T(8,128)S(1)} %multiply_bitcast_fusion.1, f32[16,1,128,128]{2,3,0,1:T(8,128)S(1)} %copy-done.7, ...), kind=kOutput, calls=%fused_computation.34 | convolution fusion | flops 6452928512 | bytes 16941056 | tf_op jit(solution)/shard_map/ihld,hlde->ihe/dot_general | solution.py:79
  328.5 2.3 bitcast_multiply_fusion.1
  330.8 31.7 %fusion.54 = f32[512,2048]{1,0:T(8,128)} fusion(f32[512,2048]{0,1:T(8,128)} %bitcast_multiply_fusion.1, f32[2048,2048]{1,0:T(8,128)} %all-gather.3.cloned.1.call-done), kind=kOutput, calls=%fused_computation.92 | convolution fusion | flops 25769803776 | bytes 25165824 | tf_op jit(solution)/shard_map/dot_general | solution.py:83
  362.5 10.4 %reduce-scatter.2.cloned.1.call-done = f32[512,1024]{1,0:T(8,128)} async-done(((f32[512,2048]{1,0:T(8,128)}), f32[512,1024]{1,0:T(8,128)}) %reduce-scatter.2.cloned.1.call-update) | async-done | bytes 2097168 | tf_op jit(solution)/shard_map/reduce_scatter | solution.py:89
  (79 shorter events, 6.0 us)
Async XLA Ops:
  6.5 0.8 copy-start
  6.5 324.3 %all-gather.3.cloned.1.call-start = ((), (), s32[]{:S(2)}) async-start(), calls=%async_computation.1 | async-start | bytes 17825792 | tf_op jit(solution)/shard_map/all_gather | solution.py:85
  7.3 365.7 %reduce-scatter.2.cloned.1.call-start = ((), (), s32[]{:S(2)}) async-start(), calls=%async_computation.2 | async-start | bytes 6291456 | tf_op jit(solution)/shard_map/reduce_scatter | solution.py:89
  15.0 10.8 %copy-start.11 = (u32[32]{0:T(128)S(1)}, u32[32]{0:T(128)}, u32[]{:S(2)}) copy-start(u32[32]{0:T(128)} %constant.67) | copy-start | bytes 388
  22.8 78.0 %slice-start = ((f32[16,14,512]{2,0,1:T(8,128)}), f32[16,10,512]{2,0,1:T(8,128)S(1)}, s32[]{:S(2)}) async-start(f32[16,14,512]{2,0,1:T(8,128)} %param.13), calls=%async_computation.3 | async-start | bytes 655360 | tf_op jit(solution)/shard_map/slice | solution.py:52
  22.8 76.6 %collective-permute-start.1 = (f32[16,128,128]{1,2,0:T(8,128)S(1)}, f32[16,128,128]{1,2,0:T(8,128)S(1)}, u32[]{:S(2)}, u32[]{:S(2)}) collective-permute-start(f32[16,128,128]{1,2,0:T(8,128)S(1)} %fusion.36), channel_id=1, source_target_pairs={{0,2},{2,0},{4,6},{6,4},{8,10},{10,8},{12,14},{14,12},{16,18},{18,... | collective-permute-start | bytes 3145736 | tf_op jit(solution)/shard_map/ppermute | solution.py:25
  92.3 3.6 collective-permute-start
  95.9 3.6 collective-permute-start.2
  100.7 24.2 %collective-permute-start.3 = (f32[16,128,128]{1,2,0:T(8,128)S(1)}, f32[16,128,128]{1,2,0:T(8,128)S(1)}, u32[]{:S(2)}, u32[]{:S(2)}) collective-permute-start(f32[16,128,128]{1,2,0:T(8,128)S(1)} %get-tuple-element.115), channel_id=1, source_target_pairs={{0,4},{2,6},{4,0},{6,2},{8,12},{10,14},{12,8},{14,10},{16,20},{18,... | collective-permute-start | bytes 3145736 | tf_op jit(solution)/shard_map/ppermute | solution.py:25
  125.0 4.4 %copy-start.2 = (f32[16,10,512]{1,0,2:T(8,128)S(1)}, f32[16,10,512]{1,0,2:T(8,128)}, u32[]{:S(2)}) copy-start(f32[16,10,512]{1,0,2:T(8,128)} %copy.29) | copy-start | bytes 983044
  125.0 1.0 copy-start.8
  129.4 81.1 %collective-permute-start.5 = (f32[16,128,128]{1,2,0:T(8,128)S(1)}, f32[16,128,128]{1,2,0:T(8,128)S(1)}, u32[]{:S(2)}, u32[]{:S(2)}) collective-permute-start(f32[16,128,128]{1,2,0:T(8,128)S(1)} %get-tuple-element.117), channel_id=1, source_target_pairs={{0,8},{2,10},{4,12},{6,14},{8,0},{10,2},{12,4},{14,6},{16,24},{18,... | collective-permute-start | bytes 3145736 | tf_op jit(solution)/shard_map/ppermute | solution.py:25
  142.1 51.7 %collective-permute-start.4 = (f32[16]{0:T(128)S(1)}, f32[16]{0:T(128)S(1)}, u32[]{:S(2)}, u32[]{:S(2)}) collective-permute-start(f32[16]{0:T(128)S(1)} %get-tuple-element.125), channel_id=1, source_target_pairs={{0,8},{2,10},{4,12},{6,14},{8,0},{10,2},{12,4},{14,6},{16,24},{18,... | collective-permute-start | bytes 200 | tf_op jit(solution)/shard_map/ppermute | solution.py:25
  193.8 16.6 %collective-permute-start.6 = (f32[16]{0:T(128)S(1)}, f32[16]{0:T(128)S(1)}, u32[]{:S(2)}, u32[]{:S(2)}) collective-permute-start(f32[16]{0:T(128)S(1)} %get-tuple-element.109), channel_id=1, source_target_pairs={{0,16},{2,18},{4,20},{6,22},{8,24},{10,26},{12,28},{14,30},{16,0},... | collective-permute-start | bytes 200 | tf_op jit(solution)/shard_map/ppermute | solution.py:25
  212.2 38.6 %copy-start.4 = (f32[16,14,512]{2,0,1:T(8,128)S(1)}, f32[16,14,512]{2,0,1:T(8,128)}, u32[]{:S(2)}) copy-start(f32[16,14,512]{2,0,1:T(8,128)} %param.13) | copy-start | bytes 1376260
  212.2 38.6 %copy-start.9 = (f32[16,512]{1,0:T(8,128)S(1)}, f32[16,512]{1,0:T(8,128)}, u32[]{:S(2)}) copy-start(f32[16,512]{1,0:T(8,128)} %get-tuple-element.121) | copy-start | bytes 98308
  212.2 93.2 %collective-permute-start.7 = (f32[16,128,128]{1,2,0:T(8,128)}, f32[16,128,128]{1,2,0:T(8,128)S(1)}, u32[]{:S(2)}, u32[]{:S(2)}) collective-permute-start(f32[16,128,128]{1,2,0:T(8,128)} %get-tuple-element.119), channel_id=1, source_target_pairs={{0,16},{2,18},{4,20},{6,22},{8,24},{10,26},{12,28},{14,30},{16,0},... | collective-permute-start | bytes 3145736 | tf_op jit(solution)/shard_map/ppermute | solution.py:25
  250.8 54.7 %copy-start.3 = (f32[16,512,128]{1,2,0:T(8,128)S(1)}, f32[16,512,128]{1,2,0:T(8,128)}, u32[]{:S(2)}) copy-start(f32[16,512,128]{1,2,0:T(8,128)} %fusion.1) | copy-start | bytes 12582916
  250.8 54.7 %copy-start.5 = (f32[16,1,128,128]{2,3,0,1:T(8,128)S(1)}, f32[16,1,128,128]{2,3,0,1:T(8,128)}, u32[]{:S(2)}) copy-start(f32[16,1,128,128]{2,3,0,1:T(8,128)} %get-tuple-element.114) | copy-start | bytes 3145732
  250.8 54.7 %copy-start.6 = (f32[16,1,128,128]{2,3,0,1:T(8,128)S(1)}, f32[16,1,128,128]{2,3,0,1:T(8,128)}, u32[]{:S(2)}) copy-start(f32[16,1,128,128]{2,3,0,1:T(8,128)} %get-tuple-element.116) | copy-start | bytes 3145732
  250.8 54.7 %copy-start.7 = (f32[16,1,128,128]{2,3,0,1:T(8,128)S(1)}, f32[16,1,128,128]{2,3,0,1:T(8,128)}, u32[]{:S(2)}) copy-start(f32[16,1,128,128]{2,3,0,1:T(8,128)} %get-tuple-element.118) | copy-start | bytes 3145732
  327.7 0.9 copy-start.10
  330.8 42.1 %copy-start.1 = (f32[16,512]{1,0:T(8,128)S(1)}, f32[16,512]{1,0:T(8,128)}, u32[]{:S(2)}) copy-start(f32[16,512]{1,0:T(8,128)} %param.12) | copy-start | bytes 98308
Sparse Core Ops, SparseCore 0:
  10.1 313.3 all-gather.2
  362.7 10.2 reduce-scatter.1
where the time goes:
time: 385 us; the launch traced here: 380 us
  waiting for transfers between devices  136 us (35%)
  matrix products  132 us (34%)
  blocking collectives  64.2 us (17%)
  other arithmetic  16.1 us (4%)
  between operations  14.5 us (4%)
  local copies, waits for them, and re-layouts  11.5 us (3%)
  starting transfers between devices  5.18 us (1%)
    ppermute x8, waiting for transfers between devices, from_partner(): return lax.ppermute(value, axis, pairs)  125 us
    unnamed x1, blocking collectives  64.2 us
    dot_general x1, matrix products, local(): local_out = jnp.einsum('hij,jhd->ihd', scores, value_heads, precision=HIGH)  38.5 us
    dot_general x1, matrix products, local(): jnp.dot(normed, lax.all_gather(out_weight, 'seq', axis=1, tiled=True), pr...  31.7 us
    dot_general x1, matrix products, local(): far_out = jnp.einsum('ihld,hlde->ihe', weighted, stacked, precision=HIGH)  22.1 us
    dot_general x1, matrix products, local(): jnp.einsum('ihd,jhd->hij', query_heads, key_heads, precision=HIGH) * near  19.2 us
    dot_general x1, matrix products, local(): jnp.einsum('hli,lij->hij', level_weights[:, :tok_bits + 1, :], onehot, pr...  12.7 us
    reduce_scatter x1, waiting for transfers between devices, local(): return lax.psum_scatter(partials, 'head', scatter_dimension=1, tiled=True)  10.4 us
  transfers between devices with their start and end apart: 10, of which 6 were waited for; matrix products, arithmetic and copies ran while one was open for 33% of the time, Pallas kernels for 0%

commit v1 on v0

v1 whole, which is shorter than its diff:
```python
import functools

import jax
import jax.numpy as jnp
from jax import lax
from jax.experimental import pallas as pl
from jax.experimental.pallas import tpu as pltpu
from jax.sharding import PartitionSpec as P

LANES = 128
PAD_ROWS = 8
VMEM_LIMIT = 48 * 1024 * 1024


def split(x):
    high = x.astype(jnp.bfloat16)
    low = (x - high.astype(jnp.float32)).astype(jnp.bfloat16)
    return high, low


def mm(a, b):
    return jnp.dot(a, b, preferred_element_type=jnp.float32)


def dot3(a, b):
    (ah, al), (bh, bl) = split(a), split(b)
    return mm(ah, bh) + (mm(al, bh) + mm(ah, bl))


def params():
    return pltpu.CompilerParams(vmem_limit_bytes=VMEM_LIMIT)


def state_kernel(k_ref, v_ref, c_ref, o_ref):
    c = c_ref[0]
    end = c[:, -1:]
    size = k_ref.shape[1]
    o_ref[0, :size, :] = dot3(v_ref[...].T * jnp.exp(end - c), k_ref[...])
    o_ref[0, size:, :] = jnp.broadcast_to(end, (PAD_ROWS, size))


def near_kernel(base_bits, tok_bits, q_ref, k_ref, v_ref, c_ref, w_ref, o_ref):
    size = q_ref.shape[1]
    base = 1 << base_bits
    tok_count = q_ref.shape[0]
    q_t = (q_ref[...] * size ** (-0.5)).T
    v_t = v_ref[...].T
    rows = lax.broadcasted_iota(jnp.int32, (base, base), 0)
    cols = lax.broadcasted_iota(jnp.int32, (base, base), 1)
    mixed = rows ^ cols
    for block in range(tok_count // base):
        at = slice(block * base, (block + 1) * base)
        c = c_ref[0, :, at]
        column = jnp.broadcast_to(c, (base, base)).T
        weight = jnp.broadcast_to(w_ref[0, 0:1, at], (base, base))
        for bit in range(base_bits):
            weight = jnp.where(mixed >> bit > 0, w_ref[0, bit + 1 : bit + 2, at], weight)
        gap = jnp.where(cols >= rows, c - column, -jnp.inf)
        scores = dot3(k_ref[at, :], q_t[:, at]) * weight * jnp.exp(gap)
        total = dot3(v_t[:, at], scores)
        o_ref[0, :, at] = total
    for bit in range(base_bits, tok_bits):
        span = 1 << bit
        for pair in range(tok_count // (2 * span)):
            low = slice(2 * pair * span, (2 * pair + 1) * span)
            high = slice((2 * pair + 1) * span, (2 * pair + 2) * span)
            c_low, c_high = c_ref[0, :, low], c_ref[0, :, high]
            end = c_low[:, -1:]
            state = dot3(v_t[:, low] * jnp.exp(end - c_low), k_ref[low, :])
            weight = w_ref[0, bit + 1 : bit + 2, high] * jnp.exp(c_high - end)
            o_ref[0, :, high] += dot3(state, q_t[:, high] * weight)


def far_kernel(levels, q_ref, near_ref, w_ref, gain_ref, *refs):
    states, (high_ref, low_ref) = refs[:levels], refs[levels:]
    size = q_ref.shape[1]
    q_t = (q_ref[...] * size ** (-0.5)).T
    total = near_ref[0]
    for level in range(levels):
        total += dot3(states[level][0, :size, :], q_t * w_ref[0, level : level + 1, :])
    mean = jnp.mean(total * total, axis=0, keepdims=True)
    normed = (total / jnp.sqrt(mean + 1e-06)).T * gain_ref[...]
    high, low = split(normed)
    high_ref[...] = high
    low_ref[...] = low


def project_kernel(places_ref, high_ref, low_ref, *refs):
    pieces, out_ref = refs[:5], refs[-1]
    width = pieces[0].shape[1]
    high, low = high_ref[...], low_ref[...]

    def product(left_high, left_low, right):
        right_high, right_low = split(right)
        return mm(left_high, right_high) + (mm(left_low, right_high) + mm(left_high, right_low))

    def put(index, value):
        start = pl.multiple_of(places_ref[1 + index] * width, width)
        out_ref[:, pl.ds(start, width)] = value

    first = jnp.concatenate([pieces[0][...], pieces[1][...]], axis=1)
    result = product(high, low, first)
    put(0, result[:, :width])
    put(1, result[:, width:])
    corner = jnp.concatenate([pieces[3][...], pieces[4][...]], axis=0)
    second = jnp.concatenate([pieces[2][...], corner], axis=1)
    result = product(high, low, second)
    put(2, result[:, :width])
    put(3, result[:, width:])


def plain_kernel(high_ref, low_ref, w_ref, o_ref):
    right_high, right_low = split(w_ref[...])
    high = high_ref[...]
    o_ref[...] = mm(high, right_high) + (mm(low_ref[...], right_high) + mm(high, right_low))


def from_partner(value, mask):
    pairs = [(source, source ^ mask) for source in range(lax.axis_size("seq"))]
    return lax.ppermute(value, "seq", pairs)


def local(queries, keys, values, log_decay, level_weights, norm_gain, out_weight):
    head_count, tok_count = log_decay.shape
    feature_count = queries.shape[1]
    size = feature_count // head_count
    tok_bits = tok_count.bit_length() - 1
    seq_size = lax.axis_size("seq")
    seq_bits = seq_size.bit_length() - 1
    seq_index = lax.axis_index("seq")
    head_size, head_index = lax.axis_size("head"), lax.axis_index("head")
    width = out_weight.shape[1]
    spread = width % LANES == 0 and seq_bits >= 2

    groups = []
    if spread:
        half = feature_count // 2
        for step in range(seq_size // 4):
            own = out_weight if step == 0 else from_partner(out_weight, 4 * step)
            groups.append([own])
        for step, group in enumerate(groups):
            own = group[0]
            by_x, by_y = from_partner(own, 1), from_partner(own, 2)
            corner_low = from_partner(by_x[:half], 2)
            corner_high = from_partner(by_y[half:], 1)
            group += [by_x, by_y, corner_low, corner_high]

    decay_sum = jnp.cumsum(log_decay, axis=1)
    decay_rows = decay_sum[:, None, :]
    tok_spec = pl.BlockSpec((tok_count, size), lambda h: (0, h))
    row_spec = pl.BlockSpec((1, 1, tok_count), lambda h: (h, 0, 0))
    state_spec = pl.BlockSpec((1, size + PAD_ROWS, size), lambda h: (h, 0, 0))
    out_spec = pl.BlockSpec((1, size, tok_count), lambda h: (h, 0, 0))
    state_flops = 6 * feature_count * tok_count * size
    call_state = pl.pallas_call(
        state_kernel,
        grid=(head_count,),
        in_specs=[tok_spec, tok_spec, row_spec],
        out_specs=state_spec,
        out_shape=jax.ShapeDtypeStruct((head_count, size + PAD_ROWS, size), jnp.float32),
        compiler_params=params(),
        cost_estimate=pl.CostEstimate(
            flops=state_flops,
            bytes_accessed=2 * keys.size * 4,
            transcendentals=head_count * tok_count,
        ),
        name="own_state",
    )
    own_state = call_state(keys, values, decay_rows)

    near_levels = level_weights[:, : tok_bits + 1, :]
    base_bits = min(LANES.bit_length() - 1, tok_bits)
    call_near = pl.pallas_call(
        functools.partial(near_kernel, base_bits, tok_bits),
        grid=(head_count,),
        in_specs=[
            tok_spec,
            tok_spec,
            tok_spec,
            row_spec,
            pl.BlockSpec((1, tok_bits + 1, tok_count), lambda h: (h, 0, 0)),
        ],
        out_specs=out_spec,
        out_shape=jax.ShapeDtypeStruct((head_count, size, tok_count), jnp.float32),
        compiler_params=params(),
        cost_estimate=pl.CostEstimate(
            flops=16 * state_flops,
            bytes_accessed=4 * keys.size * 4,
            transcendentals=head_count * tok_count * LANES,
        ),
        name="near",
    )
    near = call_near(queries, keys, values, decay_rows, near_levels)

    block = own_state
    inside = jnp.zeros((head_count,), jnp.float32)
    states, reaches = [], []
    for level_bit in range(seq_bits):
        other = from_partner(block, 2**level_bit)
        is_upper = seq_index >> level_bit & 1 == 1
        states.append(other)
        reaches.append(jnp.where(is_upper, jnp.exp(inside), 0.0))
        other_decay = other[:, size, 0]
        inside = jnp.where(is_upper, inside + other_decay, inside)
        if level_bit < seq_bits - 1:
            mine_decay = block[:, size:, :]
            decay_other = other[:, size:, :]
            late = jnp.where(is_upper, mine_decay, decay_other)[:, :1, :]
            low = jnp.where(is_upper, other, block)[:, :size, :]
            high = jnp.where(is_upper, block, other)[:, :size, :]
            merged = jnp.exp(late) * low + high
            block = jnp.concatenate([merged, mine_decay + decay_other], axis=1)
    far_weight = (
        level_weights[:, tok_bits + 1 :, :]
        * jnp.exp(decay_sum)[:, None, :]
        * jnp.stack(reaches, axis=1)[:, :, None]
    )
    call_far = pl.pallas_call(
        functools.partial(far_kernel, seq_bits),
        grid=(head_count,),
        in_specs=[
            tok_spec,
            out_spec,
            pl.BlockSpec((1, seq_bits, tok_count), lambda h: (h, 0, 0)),
            pl.BlockSpec((1, size), lambda h: (0, h)),
        ]
        + [state_spec] * seq_bits,
        out_specs=[tok_spec, tok_spec],
        out_shape=[jax.ShapeDtypeStruct((tok_count, feature_count), jnp.bfloat16)] * 2,
        compiler_params=params(),
        cost_estimate=pl.CostEstimate(
            flops=seq_bits * state_flops,
            bytes_accessed=3 * keys.size * 4,
            transcendentals=0,
        ),
        name="far",
    )
    normed_high, normed_low = call_far(
        queries, near, far_weight, norm_gain[None, :], *states
    )

    column_count = width * seq_size
    partial_shape = jax.ShapeDtypeStruct((tok_count, column_count), jnp.float32)
    whole = pl.BlockSpec(memory_space=pltpu.VMEM)
    if spread:
        partials = None
        low_bits = seq_index & 3
        for step, group in enumerate(groups):
            places = jnp.stack([(seq_index >> 2) ^ step] + [low_bits ^ e for e in range(4)])
            full = lambda rows, columns: pl.BlockSpec((rows, columns), lambda i, p: (0, 0))
            carried = [] if partials is None else [partials]
            partials = pl.pallas_call(
                project_kernel,
                grid_spec=pltpu.PrefetchScalarGridSpec(
                    num_scalar_prefetch=1,
                    grid=(1,),
                    in_specs=[full(tok_count, feature_count)] * 2
                    + [full(*piece.shape) for piece in group]
                    + [pl.BlockSpec(memory_space=pl.ANY)] * len(carried),
                    out_specs=pl.BlockSpec((tok_count, 4 * width), lambda i, p: (0, p[0])),
                ),
                out_shape=partial_shape,
                input_output_aliases={8: 0} if carried else {},
                compiler_params=params(),
                cost_estimate=pl.CostEstimate(
                    flops=6 * tok_count * feature_count * 4 * width,
                    bytes_accessed=4 * (feature_count * 4 * width + 2 * tok_count * feature_count),
                    transcendentals=0,
                ),
                name="project",
            )(places.astype(jnp.int32), normed_high, normed_low, *group, *carried)
    else:
        gathered = lax.all_gather(out_weight, "seq", axis=1, tiled=True)
        step = min(4 * LANES, column_count)
        partials = pl.pallas_call(
            plain_kernel,
            grid=(column_count // step,),
            in_specs=[
                pl.BlockSpec((tok_count, feature_count), lambda i: (0, 0)),
                pl.BlockSpec((tok_count, feature_count), lambda i: (0, 0)),
                pl.BlockSpec((feature_count, step), lambda i: (0, i)),
            ],
            out_specs=pl.BlockSpec((tok_count, step), lambda i: (0, i)),
            out_shape=partial_shape,
            compiler_params=params(),
            name="project",
        )(normed_high, normed_low, gathered)
    if head_size != 2:
        return lax.psum_scatter(partials, "head", scatter_dimension=1, tiled=True)
    share = column_count // 2
    sent = lax.dynamic_slice(partials, (0, (1 - head_index) * share), (tok_count, share))
    kept = lax.dynamic_slice(partials, (0, head_index * share), (tok_count, share))
    return kept + lax.ppermute(sent, "head", [(0, 1), (1, 0)])


def solution(mesh):
    return jax.shard_map(
        local,
        mesh=mesh,
        in_specs=(
            P("seq", "head"),
            P("seq", "head"),
            P("seq", "head"),
            P("head", "seq"),
            P("head", None, "seq"),
            P("head"),
            P("head", "seq"),
        ),
        out_specs=P("seq", "head"),
        check_vma=False,
    )
```

time: 385 us -> 301 us (0.78)
  the two profiles are of different devices: /device:TPU:0 before, /device:TPU:11 now
where the time goes in v1:
time: 301 us; the launch traced here: 299 us
  waiting for transfers between devices  131 us (44%)
  Pallas kernels  79.9 us (27%)
  starting transfers between devices  50.4 us (17%)
  local copies, waits for them, and re-layouts  27.2 us (9%)
  other arithmetic  9.98 us (3%)
    ppermute x23, waiting for transfers between devices, from_partner(): return lax.ppermute(value, 'seq', pairs)  127 us
    pallas_call x4, Pallas kernels, local(): pl.pallas_call(project_kernel, grid_spec=pltpu.PrefetchScalarGridSpec(num...  33 us
    ppermute x23, starting transfers between devices, from_partner(): return lax.ppermute(value, 'seq', pairs)  26.3 us
    ppermute x1, starting transfers between devices, local(): return kept + lax.ppermute(sent, 'head', [(0, 1), (1, 0)])  24.1 us
    pallas_call x1, Pallas kernels, local(): call_far(queries, near, far_weight, norm_gain[None, :], *states)  18.2 us
    pallas_call x1, Pallas kernels, local(): near = call_near(queries, keys, values, decay_rows, near_levels)  17.4 us
    pallas_call x1, Pallas kernels, local(): own_state = call_state(keys, values, decay_rows)  11.3 us
    slice x4, local copies, waits for them, and re-layouts, local(): corner_high = from_partner(by_y[half:], 1)  7.57 us
  transfers between devices with their start and end apart: 24, of which 7 were waited for; matrix products, arithmetic and copies ran while one was open for 7% of the time, Pallas kernels for 20%

profile of v1, /device:TPU:11, one launch (start us, length us, event | category | flops | bytes accessed | tf_op | source)
XLA Modules:
  0.0 298.9 jit_solution(12736138505663197129)
XLA Ops:
  2.2 2.2 copy-done.1
  4.4 11.3 %own_state.1 = f32[16,136,128]{2,1,0:T(8,128)S(1)} custom-call(f32[512,2048]{1,0:T(8,128)S(1)} %copy-done.1, f32[512,2048]{1,0:T(8,128)} %v_ref.3, f32[16,1,512]{2,1,0:T(1,128)S(1)} %bitcast.41), custom_call_target="tpu_custom_call" | custom-call | flops 805306368 | bytes 8388608 | tf_op jit(solution)/shard_map/own_state/pallas_call | solution.py:169
  16.0 25.2 %collective-permute-done.refs_0_ = f32[16,136,128]{2,1,0:T(8,128)S(1)} collective-permute-done((f32[16,136,128]{2,1,0:T(8,128)S(1)}, f32[16,136,128]{2,1,0:T(8,128)S(1)}, u32[]{:S(2)}, u32[]{:S(2)}) %collective-permute-start) | collective-permute-done | bytes 1114144 | tf_op jit(solution)/shard_map/ppermute | solution.py:120
  44.0 23.6 %collective-permute-done.1.refs_1_ = f32[16,136,128]{2,1,0:T(8,128)S(1)} collective-permute-done((f32[16,136,128]{2,1,0:T(8,128)}, f32[16,136,128]{2,1,0:T(8,128)S(1)}, u32[]{:S(2)}, u32[]{:S(2)}) %collective-permute-start.1) | collective-permute-done | bytes 1114144 | tf_op jit(solution)/shard_map/ppermute | solution.py:120
  71.9 2.3 collective-permute-start.9
  75.4 17.3 %collective-permute-done.19.refs_1_ = f32[2048,128]{1,0:T(8,128)S(1)} collective-permute-done((f32[2048,128]{1,0:T(8,128)}, f32[2048,128]{1,0:T(8,128)S(1)}, u32[]{:S(2)}, u32[]{:S(2)}) %collective-permute-start.19) | collective-permute-done | bytes 1048608 | tf_op jit(solution)/shard_map/ppermute | solution.py:120
  92.6 2.4 collective-permute-start.4
  95.1 41.8 %collective-permute-done.14.refs_0_ = f32[2048,128]{1,0:T(8,128)} collective-permute-done((f32[2048,128]{1,0:T(8,128)}, f32[2048,128]{1,0:T(8,128)}, u32[]{:S(2)}, u32[]{:S(2)}) %collective-permute-start.14) | collective-permute-done | bytes 1048608 | tf_op jit(solution)/shard_map/ppermute | solution.py:120
  143.2 14.8 %collective-permute-done.15.refs_1_ = f32[2048,128]{1,0:T(8,128)} collective-permute-done((f32[2048,128]{1,0:T(8,128)}, f32[2048,128]{1,0:T(8,128)}, u32[]{:S(2)}, u32[]{:S(2)}) %collective-permute-start.15) | collective-permute-done | bytes 1048608 | tf_op jit(solution)/shard_map/ppermute | solution.py:120
  159.2 5.8 %collective-permute-start.3 = (f32[16,136,128]{2,1,0:T(8,128)}, f32[16,136,128]{2,1,0:T(8,128)}, u32[]{:S(2)}, u32[]{:S(2)}) collective-permute-start(f32[16,136,128]{2,1,0:T(8,128)} %pad_maximum_fusion.2), channel_id=1, source_target_pairs={{0,16},{2,18},{4,20},{6,22},{8,24},{10,26},{12,28},{14,30},{16,0},... | collective-permute-start | bytes 3342344 | tf_op jit(solution)/shard_map/ppermute | solution.py:120
  165.1 17.4 %near.1.near_ref = f32[16,128,512]{2,1,0:T(8,128)S(1)} custom-call(f32[512,2048]{1,0:T(8,128)} %q_ref.3, f32[512,2048]{1,0:T(8,128)} %k_ref.3, f32[512,2048]{1,0:T(8,128)} %v_ref.3, f32[16,1,512]{2,1,0:T(1,128)S(1)} %bitcast.42, f32[16,10,512]{2,1,0:T(8,128)S(1)} %copy.22.w_ref), custom_call_target="tpu_custom_call" | custom-call | flops 12884901888 | bytes 16777216 | tf_op jit(solution)/shard_map/near/pallas_call | solution.py:193
  182.5 1.9 copy-done.2
  193.3 1.9 slice.144
  196.4 1.9 slice.145
  198.3 4.6 %collective-permute-done.5.refs_1_ = f32[2048,128]{1,0:T(8,128)} collective-permute-done((f32[2048,128]{1,0:T(8,128)}, f32[2048,128]{1,0:T(8,128)}, u32[]{:S(2)}, u32[]{:S(2)}) %collective-permute-start.5) | collective-permute-done | bytes 1048608 | tf_op jit(solution)/shard_map/ppermute | solution.py:120
  210.6 18.2 %far.1 = (bf16[512,2048]{1,0:T(8,128)(2,1)}, bf16[512,2048]{1,0:T(8,128)(2,1)}) custom-call(f32[512,2048]{1,0:T(8,128)} %q_ref.3, f32[16,128,512]{2,1,0:T(8,128)} %copy-done.2, f32[16,4,512]{2,1,0:T(4,128)S(1)} %fusion.2.w_ref, f32[1,2048]{1,0:T(1,128)S(1)} %bitcast.43, f32[16,136,128]{2,1,0:T(8,128)S(1)} %collective-permute-done.refs_0_, ...), custom_call_target="tpu_custom_call" | custom-call | flops 3221225472 | bytes 12582912 | tf_op jit(solution)/shard_map/far/pallas_call | solution.py:238
  230.7 8.2 %project.4.refs_5_ = f32[512,2048]{1,0:T(8,128)} custom-call(s32[5]{0:T(128)S(1)} %stack.70.places_ref, bf16[512,2048]{1,0:T(8,128)(2,1)} %get-tuple-element.7.high_ref, bf16[512,2048]{1,0:T(8,128)(2,1)} %get-tuple-element.8.low_ref, f32[2048,128]{1,0:T(8,128)} %refs_0_.1, f32[2048,128]{1,0:T(8,128)S(1)} %copy-done.4, ...), custom_call_target="tpu_custom_call" | custom-call | flops 3221225472 | bytes 12582912 | tf_op jit(solution)/shard_map/project/pallas_call | solution.py:252
  239.3 8.4 %project.5.refs_5_ = f32[512,2048]{1,0:T(8,128)} custom-call(s32[5]{0:T(128)S(1)} %stack.68.places_ref, bf16[512,2048]{1,0:T(8,128)(2,1)} %get-tuple-element.7.high_ref, bf16[512,2048]{1,0:T(8,128)(2,1)} %get-tuple-element.8.low_ref, f32[2048,128]{1,0:T(8,128)} %collective-permute-done.14.refs_0_, ...), custom_call_target="tpu_custom_call", output_to_operand_aliasing={{}: (8, {})} | custom-call | flops 3221225472 | bytes 12582912 | tf_op jit(solution)/shard_map/project/pallas_call | solution.py:252
  247.8 8.2 %project.6.refs_5_ = f32[512,2048]{1,0:T(8,128)} custom-call(s32[5]{0:T(128)S(1)} %stack.66.places_ref, bf16[512,2048]{1,0:T(8,128)(2,1)} %get-tuple-element.7.high_ref, bf16[512,2048]{1,0:T(8,128)(2,1)} %get-tuple-element.8.low_ref, f32[2048,128]{1,0:T(8,128)} %collective-permute-done.9.refs_0_, ...), custom_call_target="tpu_custom_call", output_to_operand_aliasing={{}: (8, {})} | custom-call | flops 3221225472 | bytes 12582912 | tf_op jit(solution)/shard_map/project/pallas_call | solution.py:252
  255.9 8.3 %project.7 = f32[512,2048]{1,0:T(8,128)} custom-call(s32[5]{0:T(128)S(1)} %stack.62.places_ref, bf16[512,2048]{1,0:T(8,128)(2,1)} %get-tuple-element.7.high_ref, bf16[512,2048]{1,0:T(8,128)(2,1)} %get-tuple-element.8.low_ref, f32[2048,128]{1,0:T(8,128)} %collective-permute-done.4.refs_0_, ...), custom_call_target="tpu_custom_call", output_to_operand_aliasing={{}: (8, {})} | custom-call | flops 3221225472 | bytes 12582912 | tf_op jit(solution)/shard_map/project/pallas_call | solution.py:252
  264.2 3.2 %constant_dynamic-slice_fusion = f32[512,1024]{1,0:T(8,128)} fusion(f32[512,2048]{1,0:T(8,128)} %project.7, s32[]{:T(128)S(6)} %select_n.184), kind=kLoop, calls=%fused_computation.38 | loop fusion | bytes 4194308 | tf_op jit(solution)/shard_map/dynamic_slice | solution.py:291
  267.4 24.1 %collective-permute-start.23 = (f32[512,1024]{1,0:T(8,128)}, f32[512,1024]{1,0:T(8,128)S(1)}, u32[]{:S(2)}, u32[]{:S(2)}) collective-permute-start(f32[512,1024]{1,0:T(8,128)} %constant_dynamic-slice_fusion), channel_id=1, source_target_pairs={{0,1},{1,0},{2,3},{3,2},{4,5},{5,4},{6,7},{7,6},{8,9},{9,8},{10,11... | collective-permute-start | bytes 6291464 | tf_op jit(solution)/shard_map/ppermute | solution.py:293
  291.5 4.0 %collective-permute-done.23 = f32[512,1024]{1,0:T(8,128)S(1)} collective-permute-done((f32[512,1024]{1,0:T(8,128)}, f32[512,1024]{1,0:T(8,128)S(1)}, u32[]{:S(2)}, u32[]{:S(2)}) %collective-permute-start.23) | collective-permute-done | bytes 2097184 | tf_op jit(solution)/shard_map/ppermute | solution.py:293
  295.5 3.5 %dynamic-slice_add_fusion = f32[512,1024]{1,0:T(8,128)} fusion(f32[512,1024]{1,0:T(8,128)S(1)} %collective-permute-done.23, f32[512,2048]{1,0:T(8,128)} %project.7, s32[]{:T(128)S(6)} %select_n.183), kind=kLoop, calls=%fused_computation | loop fusion | flops 524288 | bytes 6291460 | tf_op jit(solution)/shard_map/add | solution.py:293
  (101 shorter events, 38.4 us)
Async XLA Ops:
  15.7 25.5 %collective-permute-start = (f32[16,136,128]{2,1,0:T(8,128)S(1)}, f32[16,136,128]{2,1,0:T(8,128)S(1)}, u32[]{:S(2)}, u32[]{:S(2)}) collective-permute-start(f32[16,136,128]{2,1,0:T(8,128)S(1)} %own_state.1), channel_id=1, source_target_pairs={{0,2},{2,0},{4,6},{6,4},{8,10},{10,8},{12,14},{14,12},{16,18},{18,... | collective-permute-start | bytes 3342344 | tf_op jit(solution)/shard_map/ppermute | solution.py:120
  42.8 24.8 %collective-permute-start.1 = (f32[16,136,128]{2,1,0:T(8,128)}, f32[16,136,128]{2,1,0:T(8,128)S(1)}, u32[]{:S(2)}, u32[]{:S(2)}) collective-permute-start(f32[16,136,128]{2,1,0:T(8,128)} %pad_maximum_fusion), channel_id=1, source_target_pairs={{0,4},{2,6},{4,0},{6,2},{8,12},{10,14},{12,8},{14,10},{16,20},{18,... | collective-permute-start | bytes 3342344 | tf_op jit(solution)/shard_map/ppermute | solution.py:120
  70.0 67.7 %collective-permute-start.2 = (f32[16,136,128]{2,1,0:T(8,128)S(1)}, f32[16,136,128]{2,1,0:T(8,128)S(1)}, u32[]{:S(2)}, u32[]{:S(2)}) collective-permute-start(f32[16,136,128]{2,1,0:T(8,128)S(1)} %pad_maximum_fusion.1), channel_id=1, source_target_pairs={{0,8},{2,10},{4,12},{6,14},{8,0},{10,2},{12,4},{14,6},{16,24},{18,... | collective-permute-start | bytes 3342344 | tf_op jit(solution)/shard_map/ppermute | solution.py:120
  70.3 22.4 %collective-permute-start.19 = (f32[2048,128]{1,0:T(8,128)}, f32[2048,128]{1,0:T(8,128)S(1)}, u32[]{:S(2)}, u32[]{:S(2)}) collective-permute-start(f32[2048,128]{1,0:T(8,128)} %refs_0_.1), channel_id=1, source_target_pairs={{0,2},{2,0},{4,6},{6,4},{8,10},{10,8},{12,14},{14,12},{16,18},{18,... | collective-permute-start | bytes 3145736 | tf_op jit(solution)/shard_map/ppermute | solution.py:120
  70.8 66.0 %collective-permute-start.14 = (f32[2048,128]{1,0:T(8,128)}, f32[2048,128]{1,0:T(8,128)}, u32[]{:S(2)}, u32[]{:S(2)}) collective-permute-start(f32[2048,128]{1,0:T(8,128)} %refs_0_.1), channel_id=1, source_target_pairs={{0,8},{2,10},{4,12},{6,14},{8,0},{10,2},{12,4},{14,6},{16,24},{18,... | collective-permute-start | bytes 3145736 | tf_op jit(solution)/shard_map/ppermute | solution.py:120
  71.9 69.1 %collective-permute-start.9 = (f32[2048,128]{1,0:T(8,128)}, f32[2048,128]{1,0:T(8,128)}, u32[]{:S(2)}, u32[]{:S(2)}) collective-permute-start(f32[2048,128]{1,0:T(8,128)} %refs_0_.1), channel_id=1, source_target_pairs={{0,16},{2,18},{4,20},{6,22},{8,24},{10,26},{12,28},{14,30},{16,0},... | collective-permute-start | bytes 3145736 | tf_op jit(solution)/shard_map/ppermute | solution.py:120
  74.1 68.0 %collective-permute-start.20 = (f32[2048,128]{1,0:T(8,128)}, f32[2048,128]{1,0:T(8,128)}, u32[]{:S(2)}, u32[]{:S(2)}) collective-permute-start(f32[2048,128]{1,0:T(8,128)} %refs_0_.1), channel_id=1, source_target_pairs={{0,4},{2,6},{4,0},{6,2},{8,12},{10,14},{12,8},{14,10},{16,20},{18,... | collective-permute-start | bytes 3145736 | tf_op jit(solution)/shard_map/ppermute | solution.py:120
  92.6 49.7 %collective-permute-start.4 = (f32[2048,128]{1,0:T(8,128)}, f32[2048,128]{1,0:T(8,128)}, u32[]{:S(2)}, u32[]{:S(2)}) collective-permute-start(f32[2048,128]{1,0:T(8,128)} %refs_0_.1), channel_id=1, source_target_pairs={{0,24},{2,26},{4,28},{6,30},{8,16},{10,18},{12,20},{14,22},{16,8},... | collective-permute-start | bytes 3145736 | tf_op jit(solution)/shard_map/ppermute | solution.py:120
  136.9 21.1 %collective-permute-start.15 = (f32[2048,128]{1,0:T(8,128)}, f32[2048,128]{1,0:T(8,128)}, u32[]{:S(2)}, u32[]{:S(2)}) collective-permute-start(f32[2048,128]{1,0:T(8,128)} %collective-permute-done.14.refs_0_), channel_id=1, source_target_pairs={{0,2},{2,0},{4,6},{6,4},{8,10},{10,8},{12,14},{14,12},{16,18},{18,... | collective-permute-start | bytes 3145736 | tf_op jit(solution)/shard_map/ppermute | solution.py:120
  137.7 21.5 %collective-permute-start.16 = (f32[2048,128]{1,0:T(8,128)}, f32[2048,128]{1,0:T(8,128)}, u32[]{:S(2)}, u32[]{:S(2)}) collective-permute-start(f32[2048,128]{1,0:T(8,128)} %collective-permute-done.14.refs_0_), channel_id=1, source_target_pairs={{0,4},{2,6},{4,0},{6,2},{8,12},{10,14},{12,8},{14,10},{16,20},{18,... | collective-permute-start | bytes 3145736 | tf_op jit(solution)/shard_map/ppermute | solution.py:120
  140.9 52.1 %collective-permute-start.10 = (f32[2048,128]{1,0:T(8,128)}, f32[2048,128]{1,0:T(8,128)}, u32[]{:S(2)}, u32[]{:S(2)}) collective-permute-start(f32[2048,128]{1,0:T(8,128)} %collective-permute-done.9.refs_0_), channel_id=1, source_target_pairs={{0,2},{2,0},{4,6},{6,4},{8,10},{10,8},{12,14},{14,12},{16,18},{18,... | collective-permute-start | bytes 3145736 | tf_op jit(solution)/shard_map/ppermute | solution.py:120
  142.2 53.0 %collective-permute-start.11 = (f32[2048,128]{1,0:T(8,128)}, f32[2048,128]{1,0:T(8,128)}, u32[]{:S(2)}, u32[]{:S(2)}) collective-permute-start(f32[2048,128]{1,0:T(8,128)} %collective-permute-done.9.refs_0_), channel_id=1, source_target_pairs={{0,4},{2,6},{4,0},{6,2},{8,12},{10,14},{12,8},{14,10},{16,20},{18,... | collective-permute-start | bytes 3145736 | tf_op jit(solution)/shard_map/ppermute | solution.py:120
  142.4 60.5 %collective-permute-start.5 = (f32[2048,128]{1,0:T(8,128)}, f32[2048,128]{1,0:T(8,128)}, u32[]{:S(2)}, u32[]{:S(2)}) collective-permute-start(f32[2048,128]{1,0:T(8,128)} %collective-permute-done.4.refs_0_), channel_id=1, source_target_pairs={{0,2},{2,0},{4,6},{6,4},{8,10},{10,8},{12,14},{14,12},{16,18},{18,... | collective-permute-start | bytes 3145736 | tf_op jit(solution)/shard_map/ppermute | solution.py:120
  158.0 48.1 %collective-permute-start.6 = (f32[2048,128]{1,0:T(8,128)}, f32[2048,128]{1,0:T(8,128)}, u32[]{:S(2)}, u32[]{:S(2)}) collective-permute-start(f32[2048,128]{1,0:T(8,128)} %collective-permute-done.4.refs_0_), channel_id=1, source_target_pairs={{0,4},{2,6},{4,0},{6,2},{8,12},{10,14},{12,8},{14,10},{16,20},{18,... | collective-permute-start | bytes 3145736 | tf_op jit(solution)/shard_map/ppermute | solution.py:120
  159.2 50.5 %collective-permute-start.3 = (f32[16,136,128]{2,1,0:T(8,128)}, f32[16,136,128]{2,1,0:T(8,128)}, u32[]{:S(2)}, u32[]{:S(2)}) collective-permute-start(f32[16,136,128]{2,1,0:T(8,128)} %pad_maximum_fusion.2), channel_id=1, source_target_pairs={{0,16},{2,18},{4,20},{6,22},{8,24},{10,26},{12,28},{14,30},{16,0},... | collective-permute-start | bytes 3342344 | tf_op jit(solution)/shard_map/ppermute | solution.py:120
  193.1 35.7 %collective-permute-start.21 = (f32[1024,128]{1,0:T(8,128)}, f32[1024,128]{1,0:T(8,128)}, u32[]{:S(2)}, u32[]{:S(2)}) collective-permute-start(f32[1024,128]{1,0:T(8,128)} %slice.148), channel_id=1, source_target_pairs={{0,4},{2,6},{4,0},{6,2},{8,12},{10,14},{12,8},{14,10},{16,20},{18,... | collective-permute-start | bytes 1572872 | tf_op jit(solution)/shard_map/ppermute | solution.py:120
  195.2 34.3 %collective-permute-start.22 = (f32[1024,128]{1,0:T(8,128)}, f32[1024,128]{1,0:T(8,128)}, u32[]{:S(2)}, u32[]{:S(2)}) collective-permute-start(f32[1024,128]{1,0:T(8,128)} %slice.149), channel_id=1, source_target_pairs={{0,2},{2,0},{4,6},{6,4},{8,10},{10,8},{12,14},{14,12},{16,18},{18,... | collective-permute-start | bytes 1572872 | tf_op jit(solution)/shard_map/ppermute | solution.py:120
  202.9 36.0 %collective-permute-start.17 = (f32[1024,128]{1,0:T(8,128)}, f32[1024,128]{1,0:T(8,128)}, u32[]{:S(2)}, u32[]{:S(2)}) collective-permute-start(f32[1024,128]{1,0:T(8,128)} %slice.146), channel_id=1, source_target_pairs={{0,4},{2,6},{4,0},{6,2},{8,12},{10,14},{12,8},{14,10},{16,20},{18,... | collective-permute-start | bytes 1572872 | tf_op jit(solution)/shard_map/ppermute | solution.py:120
  206.1 33.3 %collective-permute-start.18 = (f32[1024,128]{1,0:T(8,128)}, f32[1024,128]{1,0:T(8,128)}, u32[]{:S(2)}, u32[]{:S(2)}) collective-permute-start(f32[1024,128]{1,0:T(8,128)} %slice.147), channel_id=1, source_target_pairs={{0,2},{2,0},{4,6},{6,4},{8,10},{10,8},{12,14},{14,12},{16,18},{18,... | collective-permute-start | bytes 1572872 | tf_op jit(solution)/shard_map/ppermute | solution.py:120
  209.8 38.0 %collective-permute-start.12 = (f32[1024,128]{1,0:T(8,128)}, f32[1024,128]{1,0:T(8,128)S(1)}, u32[]{:S(2)}, u32[]{:S(2)}) collective-permute-start(f32[1024,128]{1,0:T(8,128)} %slice.144), channel_id=1, source_target_pairs={{0,4},{2,6},{4,0},{6,2},{8,12},{10,14},{12,8},{14,10},{16,20},{18,... | collective-permute-start | bytes 1572872 | tf_op jit(solution)/shard_map/ppermute | solution.py:120
  228.8 18.9 %collective-permute-start.13 = (f32[1024,128]{1,0:T(8,128)S(1)}, f32[1024,128]{1,0:T(8,128)S(1)}, u32[]{:S(2)}, u32[]{:S(2)}) collective-permute-start(f32[1024,128]{1,0:T(8,128)S(1)} %copy-done.10), channel_id=1, source_target_pairs={{0,2},{2,0},{4,6},{6,4},{8,10},{10,8},{12,14},{14,12},{16,18},{18,... | collective-permute-start | bytes 1572872 | tf_op jit(solution)/shard_map/ppermute | solution.py:120
  229.5 26.5 %collective-permute-start.7 = (f32[1024,128]{1,0:T(8,128)S(1)}, f32[1024,128]{1,0:T(8,128)S(1)}, u32[]{:S(2)}, u32[]{:S(2)}) collective-permute-start(f32[1024,128]{1,0:T(8,128)S(1)} %copy-done.9), channel_id=1, source_target_pairs={{0,4},{2,6},{4,0},{6,2},{8,12},{10,14},{12,8},{14,10},{16,20},{18,... | collective-permute-start | bytes 1572872 | tf_op jit(solution)/shard_map/ppermute | solution.py:120
  238.9 17.0 %collective-permute-start.8 = (f32[1024,128]{1,0:T(8,128)S(1)}, f32[1024,128]{1,0:T(8,128)S(1)}, u32[]{:S(2)}, u32[]{:S(2)}) collective-permute-start(f32[1024,128]{1,0:T(8,128)S(1)} %copy-done.11), channel_id=1, source_target_pairs={{0,2},{2,0},{4,6},{6,4},{8,10},{10,8},{12,14},{14,12},{16,18},{18,... | collective-permute-start | bytes 1572872 | tf_op jit(solution)/shard_map/ppermute | solution.py:120
  267.4 28.1 %collective-permute-start.23 = (f32[512,1024]{1,0:T(8,128)}, f32[512,1024]{1,0:T(8,128)S(1)}, u32[]{:S(2)}, u32[]{:S(2)}) collective-permute-start(f32[512,1024]{1,0:T(8,128)} %constant_dynamic-slice_fusion), channel_id=1, source_target_pairs={{0,1},{1,0},{2,3},{3,2},{4,5},{5,4},{6,7},{7,6},{8,9},{9,8},{10,11... | collective-permute-start | bytes 6291464 | tf_op jit(solution)/shard_map/ppermute | solution.py:293
  (13 other events, 141.8 us)

commit v2 on v1

--- a/solution.py
+++ b/solution.py
@@ -71,13 +71,22 @@
             o_ref[0, :, high] += dot3(state, q_t[:, high] * weight)
 
 
-def far_kernel(levels, q_ref, near_ref, w_ref, gain_ref, *refs):
-    states, (high_ref, low_ref) = refs[:levels], refs[levels:]
+def far_sum(q_ref, near_ref, w_ref, states):
     size = q_ref.shape[1]
     q_t = (q_ref[...] * size ** (-0.5)).T
     total = near_ref[0]
-    for level in range(levels):
-        total += dot3(states[level][0, :size, :], q_t * w_ref[0, level : level + 1, :])
+    for level, state in enumerate(states):
+        total += dot3(state[0, :size, :], q_t * w_ref[0, level : level + 1, :])
+    return total
+
+
+def early_kernel(q_ref, near_ref, w_ref, *refs):
+    refs[-1][0] = far_sum(q_ref, near_ref, w_ref, refs[:-1])
+
+
+def far_kernel(q_ref, near_ref, w_ref, gain_ref, *refs):
+    states, (high_ref, low_ref) = refs[:-2], refs[-2:]
+    total = far_sum(q_ref, near_ref, w_ref, states)
     mean = jnp.mean(total * total, axis=0, keepdims=True)
     normed = (total / jnp.sqrt(mean + 1e-06)).T * gain_ref[...]
     high, low = split(normed)
@@ -141,8 +150,9 @@
         for step, group in enumerate(groups):
             own = group[0]
             by_x, by_y = from_partner(own, 1), from_partner(own, 2)
-            corner_low = from_partner(by_x[:half], 2)
-            corner_high = from_partner(by_y[half:], 1)
+            low_rows, high_rows = by_x[:half], by_y[half:]
+            corner_low = from_partner(low_rows, 2)
+            corner_high = from_partner(high_rows, 1)
             group += [by_x, by_y, corner_low, corner_high]
 
     decay_sum = jnp.cumsum(log_decay, axis=1)
@@ -210,33 +220,45 @@
             high = jnp.where(is_upper, block, other)[:, :size, :]
             merged = jnp.exp(late) * low + high
             block = jnp.concatenate([merged, mine_decay + decay_other], axis=1)
-    far_weight = (
-        level_weights[:, tok_bits + 1 :, :]
-        * jnp.exp(decay_sum)[:, None, :]
-        * jnp.stack(reaches, axis=1)[:, :, None]
-    )
+    far_levels = level_weights[:, tok_bits + 1 :, :]
+    fade = jnp.exp(decay_sum)[:, None, :]
+
+    def far_rows(first, last):
+        reach = jnp.stack(reaches[first:last], axis=1)[:, :, None]
+        return far_levels[:, first:last, :] * fade * reach
+
+    def weight_spec(count):
+        return pl.BlockSpec((1, count, tok_count), lambda h: (h, 0, 0))
+
+    last = seq_bits - 1
+    call_early = pl.pallas_call(
+        early_kernel,
+        grid=(head_count,),
+        in_specs=[tok_spec, out_spec, weight_spec(last)] + [state_spec] * last,
+        out_specs=out_spec,
+        out_shape=jax.ShapeDtypeStruct((head_count, size, tok_count), jnp.float32),
+        compiler_params=params(),
+        cost_estimate=pl.CostEstimate(
+            flops=last * state_flops, bytes_accessed=3 * keys.size * 4, transcendentals=0
+        ),
+        name="early",
+    )
+    early = call_early(queries, near, far_rows(0, last), *states[:last])
     call_far = pl.pallas_call(
-        functools.partial(far_kernel, seq_bits),
+        far_kernel,
         grid=(head_count,),
-        in_specs=[
-            tok_spec,
-            out_spec,
-            pl.BlockSpec((1, seq_bits, tok_count), lambda h: (h, 0, 0)),
-            pl.BlockSpec((1, size), lambda h: (0, h)),
-        ]
-        + [state_spec] * seq_bits,
+        in_specs=[tok_spec, out_spec, weight_spec(1), pl.BlockSpec((1, size), lambda h: (0, h))]
+        + [state_spec],
         out_specs=[tok_spec, tok_spec],
         out_shape=[jax.ShapeDtypeStruct((tok_count, feature_count), jnp.bfloat16)] * 2,
         compiler_params=params(),
         cost_estimate=pl.CostEstimate(
-            flops=seq_bits * state_flops,
-            bytes_accessed=3 * keys.size * 4,
-            transcendentals=0,
+            flops=state_flops, bytes_accessed=3 * keys.size * 4, transcendentals=0
         ),
         name="far",
     )
     normed_high, normed_low = call_far(
-        queries, near, far_weight, norm_gain[None, :], *states
+        queries, early, far_rows(last, seq_bits), norm_gain[None, :], states[last]
     )
 
     column_count = width * seq_size

time: 301 us -> 291 us (0.967)
  the two profiles are of different devices: /device:TPU:11 before, /device:TPU:0 now
where the time goes in v2:
time: 291 us; the launch traced here: 289 us
  waiting for transfers between devices  114 us (39%)
  Pallas kernels  90.4 us (31%)
  starting transfers between devices  47.4 us (16%)
  local copies, waits for them, and re-layouts  26.7 us (9%)
  other arithmetic  10.6 us (4%)
    ppermute x23, waiting for transfers between devices, from_partner(): return lax.ppermute(value, 'seq', pairs)  109 us
    ppermute x23, starting transfers between devices, from_partner(): return lax.ppermute(value, 'seq', pairs)  47.4 us
    pallas_call x4, Pallas kernels, local(): pl.pallas_call(project_kernel, grid_spec=pltpu.PrefetchScalarGridSpec(num...  31.6 us
    pallas_call x1, Pallas kernels, local(): near = call_near(queries, keys, values, decay_rows, near_levels)  17.4 us
    pallas_call x1, Pallas kernels, local(): early = call_early(queries, near, far_rows(0, last), *states[:last])  15.6 us
    pallas_call x1, Pallas kernels, local(): call_far(queries, early, far_rows(last, seq_bits), norm_gain[None, :], st...  14.5 us
    pallas_call x1, Pallas kernels, local(): own_state = call_state(keys, values, decay_rows)  11.3 us
    unnamed x57, local copies, waits for them, and re-layouts  10.6 us
  transfers between devices with their start and end apart: 24, of which 6 were waited for; matrix products, arithmetic and copies ran while one was open for 7% of the time, Pallas kernels for 25%

profile of v2, /device:TPU:0, one launch (start us, length us, event | category | flops | bytes accessed | tf_op | source)
XLA Modules:
  0.0 289.0 jit_solution(9033597448951095009)
XLA Ops:
  2.2 2.2 copy-done.4
  4.4 11.3 %own_state.1 = f32[16,136,128]{2,1,0:T(8,128)S(1)} custom-call(f32[512,2048]{1,0:T(8,128)S(1)} %copy-done.4, f32[512,2048]{1,0:T(8,128)} %v_ref.3, f32[16,1,512]{2,1,0:T(1,128)S(1)} %bitcast.31), custom_call_target="tpu_custom_call" | custom-call | flops 805306368 | bytes 8388608 | tf_op jit(solution)/shard_map/own_state/pallas_call | solution.py:179
  15.7 3.0 %collective-permute-start = (f32[16,136,128]{2,1,0:T(8,128)S(1)}, f32[16,136,128]{2,1,0:T(8,128)S(1)}, u32[]{:S(2)}, u32[]{:S(2)}) collective-permute-start(f32[16,136,128]{2,1,0:T(8,128)S(1)} %own_state.1), channel_id=1, source_target_pairs={{0,2},{2,0},{4,6},{6,4},{8,10},{10,8},{12,14},{14,12},{16,18},{18,... | collective-permute-start | bytes 3342344 | tf_op jit(solution)/shard_map/ppermute | solution.py:129
  18.8 24.6 %collective-permute-done.refs_0_ = f32[16,136,128]{2,1,0:T(8,128)S(1)} collective-permute-done((f32[16,136,128]{2,1,0:T(8,128)S(1)}, f32[16,136,128]{2,1,0:T(8,128)S(1)}, u32[]{:S(2)}, u32[]{:S(2)}) %collective-permute-start) | collective-permute-done | bytes 1114144 | tf_op jit(solution)/shard_map/ppermute | solution.py:129
  49.3 2.6 collective-permute-start.9
  52.4 17.8 %collective-permute-done.19.refs_1_ = f32[2048,128]{1,0:T(8,128)S(1)} collective-permute-done((f32[2048,128]{1,0:T(8,128)}, f32[2048,128]{1,0:T(8,128)S(1)}, u32[]{:S(2)}, u32[]{:S(2)}) %collective-permute-start.19) | collective-permute-done | bytes 1048608 | tf_op jit(solution)/shard_map/ppermute | solution.py:129
  70.2 3.6 %collective-permute-start.4 = (f32[2048,128]{1,0:T(8,128)}, f32[2048,128]{1,0:T(8,128)}, u32[]{:S(2)}, u32[]{:S(2)}) collective-permute-start(f32[2048,128]{1,0:T(8,128)} %refs_0_.1), channel_id=1, source_target_pairs={{0,24},{2,26},{4,28},{6,30},{8,16},{10,18},{12,20},{14,22},{16,8},... | collective-permute-start | bytes 3145736 | tf_op jit(solution)/shard_map/ppermute | solution.py:129
  73.8 19.0 %collective-permute-done.14.refs_0_ = f32[2048,128]{1,0:T(8,128)} collective-permute-done((f32[2048,128]{1,0:T(8,128)}, f32[2048,128]{1,0:T(8,128)}, u32[]{:S(2)}, u32[]{:S(2)}) %collective-permute-start.14) | collective-permute-done | bytes 1048608 | tf_op jit(solution)/shard_map/ppermute | solution.py:129
  95.9 2.0 copy.31.w_ref
  100.3 20.7 %collective-permute-done.9.refs_0_ = f32[2048,128]{1,0:T(8,128)} collective-permute-done((f32[2048,128]{1,0:T(8,128)}, f32[2048,128]{1,0:T(8,128)}, u32[]{:S(2)}, u32[]{:S(2)}) %collective-permute-start.9) | collective-permute-done | bytes 1048608 | tf_op jit(solution)/shard_map/ppermute | solution.py:129
  121.6 2.0 collective-permute-start.5
  125.1 18.3 %collective-permute-start.2 = (f32[16,136,128]{2,1,0:T(8,128)S(1)}, f32[16,136,128]{2,1,0:T(8,128)S(1)}, u32[]{:S(2)}, u32[]{:S(2)}) collective-permute-start(f32[16,136,128]{2,1,0:T(8,128)S(1)} %pad_maximum_fusion.1), channel_id=1, source_target_pairs={{0,8},{2,10},{4,12},{6,14},{8,0},{10,2},{12,4},{14,6},{16,24},{18,... | collective-permute-start | bytes 3342344 | tf_op jit(solution)/shard_map/ppermute | solution.py:129
  143.3 17.4 %near.1.near_ref = f32[16,128,512]{2,1,0:T(8,128)S(1)} custom-call(f32[512,2048]{1,0:T(8,128)} %q_ref.5, f32[512,2048]{1,0:T(8,128)} %k_ref.3, f32[512,2048]{1,0:T(8,128)} %v_ref.3, f32[16,1,512]{2,1,0:T(1,128)S(1)} %bitcast.32, f32[16,10,512]{2,1,0:T(8,128)S(1)} %copy-done.20), custom_call_target="tpu_custom_call" | custom-call | flops 12884901888 | bytes 16777216 | tf_op jit(solution)/shard_map/near/pallas_call | solution.py:203
  160.7 2.0 copy-done.5
  182.3 15.6 %early.1.near_ref = f32[16,128,512]{2,1,0:T(8,128)} custom-call(f32[512,2048]{1,0:T(8,128)} %q_ref.5, f32[16,128,512]{2,1,0:T(8,128)} %copy-done.5, f32[16,3,512]{2,1,0:T(4,128)S(1)} %fusion.2.w_ref, f32[16,136,128]{2,1,0:T(8,128)S(1)} %collective-permute-done.refs_0_, f32[16,136,128]{2,1,0:T(8,128)S(1)} %collective-permute-done.1.refs_1_, ...), custom_call_target="tpu_custom_call" | custom-call | flops 2415919104 | bytes 12582912 | tf_op jit(solution)/shard_map/early/pallas_call | solution.py:246
  197.9 27.1 %collective-permute-done.3.refs_0_ = f32[16,136,128]{2,1,0:T(8,128)} collective-permute-done((f32[16,136,128]{2,1,0:T(8,128)}, f32[16,136,128]{2,1,0:T(8,128)}, u32[]{:S(2)}, u32[]{:S(2)}) %collective-permute-start.3) | collective-permute-done | bytes 1114144 | tf_op jit(solution)/shard_map/ppermute | solution.py:129
  225.8 14.5 %far.1 = (bf16[512,2048]{1,0:T(8,128)(2,1)S(1)}, bf16[512,2048]{1,0:T(8,128)(2,1)S(1)}) custom-call(f32[512,2048]{1,0:T(8,128)} %q_ref.5, f32[16,128,512]{2,1,0:T(8,128)} %early.1.near_ref, f32[16,1,512]{2,1,0:T(1,128)S(1)} %fusion.3.w_ref, f32[1,2048]{1,0:T(1,128)S(1)} %bitcast.34, f32[16,136,128]{2,1,0:T(8,128)} %collective-permute-done.3.refs_0_), custom_call_target="tpu_custom_call" | custom-call | flops 805306368 | bytes 12582912 | tf_op jit(solution)/shard_map/far/pallas_call | solution.py:260
  245.3 8.1 %project.4.refs_5_ = f32[512,2048]{1,0:T(8,128)} custom-call(s32[5]{0:T(128)S(1)} %stack.69.places_ref, bf16[512,2048]{1,0:T(8,128)(2,1)} %copy-done.2, bf16[512,2048]{1,0:T(8,128)(2,1)} %copy-done.3, f32[2048,128]{1,0:T(8,128)} %refs_0_.1, f32[2048,128]{1,0:T(8,128)S(1)} %copy-done.8, f32[2048,128]{1,0:T(8,128)} %collective-permute-done.20.refs_2_, ...), custom_call_target="tpu_custom_call" | custom-call | flops 3221225472 | bytes 12582912 | tf_op jit(solution)/shard_map/project/pallas_call | solution.py:274
  254.5 8.2 %project.5.refs_5_ = f32[512,2048]{1,0:T(8,128)} custom-call(s32[5]{0:T(128)S(1)} %stack.67.places_ref, bf16[512,2048]{1,0:T(8,128)(2,1)} %copy-done.2, bf16[512,2048]{1,0:T(8,128)(2,1)} %copy-done.3, f32[2048,128]{1,0:T(8,128)} %collective-permute-done.14.refs_0_, f32[2048,128]{1,0:T(8,128)S(1)} %copy-done.11, ...), custom_call_target="tpu_custom_call", output_to_operand_aliasing={{}: (8, {})} | custom-call | flops 3221225472 | bytes 12582912 | tf_op jit(solution)/shard_map/project/pallas_call | solution.py:274
  262.7 7.6 %project.6.refs_5_ = f32[512,2048]{1,0:T(8,128)} custom-call(s32[5]{0:T(128)S(1)} %stack.65.places_ref, bf16[512,2048]{1,0:T(8,128)(2,1)} %copy-done.2, bf16[512,2048]{1,0:T(8,128)(2,1)} %copy-done.3, f32[2048,128]{1,0:T(8,128)} %collective-permute-done.9.refs_0_, f32[2048,128]{1,0:T(8,128)S(1)} %copy-done.15, ...), custom_call_target="tpu_custom_call", output_to_operand_aliasing={{}: (8, {})} | custom-call | flops 3221225472 | bytes 12582912 | tf_op jit(solution)/shard_map/project/pallas_call | solution.py:274
  270.4 7.6 %project.7 = f32[512,2048]{1,0:T(8,128)} custom-call(s32[5]{0:T(128)S(1)} %stack.61.places_ref, bf16[512,2048]{1,0:T(8,128)(2,1)} %copy-done.2, bf16[512,2048]{1,0:T(8,128)(2,1)} %copy-done.3, f32[2048,128]{1,0:T(8,128)} %collective-permute-done.4.refs_0_, f32[2048,128]{1,0:T(8,128)S(1)} %copy-done.13, ...), custom_call_target="tpu_custom_call", output_to_operand_aliasing={{}: (8, {})} | custom-call | flops 3221225472 | bytes 12582912 | tf_op jit(solution)/shard_map/project/pallas_call | solution.py:274
  278.0 3.2 %constant_dynamic-slice_fusion = f32[512,1024]{1,0:T(8,128)} fusion(f32[512,2048]{1,0:T(8,128)} %project.7, s32[]{:T(128)S(6)} %select_n.175), kind=kLoop, calls=%fused_computation.41 | loop fusion | bytes 4194308 | tf_op jit(solution)/shard_map/dynamic_slice | solution.py:313
  281.2 4.4 %collective-permute-done.23 = f32[512,1024]{1,0:T(8,128)S(1)} collective-permute-done((f32[512,1024]{1,0:T(8,128)}, f32[512,1024]{1,0:T(8,128)S(1)}, u32[]{:S(2)}, u32[]{:S(2)}) %collective-permute-start.23) | collective-permute-done | bytes 2097184 | tf_op jit(solution)/shard_map/ppermute | solution.py:315
  285.6 3.5 %dynamic-slice_add_fusion = f32[512,1024]{1,0:T(8,128)} fusion(f32[512,1024]{1,0:T(8,128)S(1)} %collective-permute-done.23, f32[512,2048]{1,0:T(8,128)} %project.7, s32[]{:T(128)S(6)} %select_n.174), kind=kLoop, calls=%fused_computation | loop fusion | flops 524288 | bytes 6291460 | tf_op jit(solution)/shard_map/add | solution.py:315
  (135 shorter events, 42.6 us)
Async XLA Ops:
  15.7 27.6 %collective-permute-start = (f32[16,136,128]{2,1,0:T(8,128)S(1)}, f32[16,136,128]{2,1,0:T(8,128)S(1)}, u32[]{:S(2)}, u32[]{:S(2)}) collective-permute-start(f32[16,136,128]{2,1,0:T(8,128)S(1)} %own_state.1), channel_id=1, source_target_pairs={{0,2},{2,0},{4,6},{6,4},{8,10},{10,8},{12,14},{14,12},{16,18},{18,... | collective-permute-start | bytes 3342344 | tf_op jit(solution)/shard_map/ppermute | solution.py:129
  44.5 49.1 %collective-permute-start.1 = (f32[16,136,128]{2,1,0:T(8,128)S(1)}, f32[16,136,128]{2,1,0:T(8,128)S(1)}, u32[]{:S(2)}, u32[]{:S(2)}) collective-permute-start(f32[16,136,128]{2,1,0:T(8,128)S(1)} %pad_maximum_fusion), channel_id=1, source_target_pairs={{0,4},{2,6},{4,0},{6,2},{8,12},{10,14},{12,8},{14,10},{16,20},{18,... | collective-permute-start | bytes 3342344 | tf_op jit(solution)/shard_map/ppermute | solution.py:129
  46.3 24.0 %collective-permute-start.19 = (f32[2048,128]{1,0:T(8,128)}, f32[2048,128]{1,0:T(8,128)S(1)}, u32[]{:S(2)}, u32[]{:S(2)}) collective-permute-start(f32[2048,128]{1,0:T(8,128)} %refs_0_.1), channel_id=1, source_target_pairs={{0,2},{2,0},{4,6},{6,4},{8,10},{10,8},{12,14},{14,12},{16,18},{18,... | collective-permute-start | bytes 3145736 | tf_op jit(solution)/shard_map/ppermute | solution.py:129
  47.8 45.1 %collective-permute-start.14 = (f32[2048,128]{1,0:T(8,128)}, f32[2048,128]{1,0:T(8,128)}, u32[]{:S(2)}, u32[]{:S(2)}) collective-permute-start(f32[2048,128]{1,0:T(8,128)} %refs_0_.1), channel_id=1, source_target_pairs={{0,8},{2,10},{4,12},{6,14},{8,0},{10,2},{12,4},{14,6},{16,24},{18,... | collective-permute-start | bytes 3145736 | tf_op jit(solution)/shard_map/ppermute | solution.py:129
  49.3 71.7 %collective-permute-start.9 = (f32[2048,128]{1,0:T(8,128)}, f32[2048,128]{1,0:T(8,128)}, u32[]{:S(2)}, u32[]{:S(2)}) collective-permute-start(f32[2048,128]{1,0:T(8,128)} %refs_0_.1), channel_id=1, source_target_pairs={{0,16},{2,18},{4,20},{6,22},{8,24},{10,26},{12,28},{14,30},{16,0},... | collective-permute-start | bytes 3145736 | tf_op jit(solution)/shard_map/ppermute | solution.py:129
  51.9 69.1 %collective-permute-start.20 = (f32[2048,128]{1,0:T(8,128)}, f32[2048,128]{1,0:T(8,128)}, u32[]{:S(2)}, u32[]{:S(2)}) collective-permute-start(f32[2048,128]{1,0:T(8,128)} %refs_0_.1), channel_id=1, source_target_pairs={{0,4},{2,6},{4,0},{6,2},{8,12},{10,14},{12,8},{14,10},{16,20},{18,... | collective-permute-start | bytes 3145736 | tf_op jit(solution)/shard_map/ppermute | solution.py:129
  70.2 51.3 %collective-permute-start.4 = (f32[2048,128]{1,0:T(8,128)}, f32[2048,128]{1,0:T(8,128)}, u32[]{:S(2)}, u32[]{:S(2)}) collective-permute-start(f32[2048,128]{1,0:T(8,128)} %refs_0_.1), channel_id=1, source_target_pairs={{0,24},{2,26},{4,28},{6,30},{8,16},{10,18},{12,20},{14,22},{16,8},... | collective-permute-start | bytes 3145736 | tf_op jit(solution)/shard_map/ppermute | solution.py:129
  92.8 30.7 %collective-permute-start.15 = (f32[2048,128]{1,0:T(8,128)}, f32[2048,128]{1,0:T(8,128)S(1)}, u32[]{:S(2)}, u32[]{:S(2)}) collective-permute-start(f32[2048,128]{1,0:T(8,128)} %collective-permute-done.14.refs_0_), channel_id=1, source_target_pairs={{0,2},{2,0},{4,6},{6,4},{8,10},{10,8},{12,14},{14,12},{16,18},{18,... | collective-permute-start | bytes 3145736 | tf_op jit(solution)/shard_map/ppermute | solution.py:129
  93.6 31.5 %collective-permute-start.16 = (f32[2048,128]{1,0:T(8,128)}, f32[2048,128]{1,0:T(8,128)}, u32[]{:S(2)}, u32[]{:S(2)}) collective-permute-start(f32[2048,128]{1,0:T(8,128)} %collective-permute-done.14.refs_0_), channel_id=1, source_target_pairs={{0,4},{2,6},{4,0},{6,2},{8,12},{10,14},{12,8},{14,10},{16,20},{18,... | collective-permute-start | bytes 3145736 | tf_op jit(solution)/shard_map/ppermute | solution.py:129
  121.0 47.2 %collective-permute-start.10 = (f32[2048,128]{1,0:T(8,128)}, f32[2048,128]{1,0:T(8,128)S(1)}, u32[]{:S(2)}, u32[]{:S(2)}) collective-permute-start(f32[2048,128]{1,0:T(8,128)} %collective-permute-done.9.refs_0_), channel_id=1, source_target_pairs={{0,2},{2,0},{4,6},{6,4},{8,10},{10,8},{12,14},{14,12},{16,18},{18,... | collective-permute-start | bytes 3145736 | tf_op jit(solution)/shard_map/ppermute | solution.py:129
  121.0 49.0 %collective-permute-start.11 = (f32[2048,128]{1,0:T(8,128)}, f32[2048,128]{1,0:T(8,128)S(1)}, u32[]{:S(2)}, u32[]{:S(2)}) collective-permute-start(f32[2048,128]{1,0:T(8,128)} %collective-permute-done.9.refs_0_), channel_id=1, source_target_pairs={{0,4},{2,6},{4,0},{6,2},{8,12},{10,14},{12,8},{14,10},{16,20},{18,... | collective-permute-start | bytes 3145736 | tf_op jit(solution)/shard_map/ppermute | solution.py:129
  121.6 50.9 %collective-permute-start.5 = (f32[2048,128]{1,0:T(8,128)}, f32[2048,128]{1,0:T(8,128)S(1)}, u32[]{:S(2)}, u32[]{:S(2)}) collective-permute-start(f32[2048,128]{1,0:T(8,128)} %collective-permute-done.4.refs_0_), channel_id=1, source_target_pairs={{0,2},{2,0},{4,6},{6,4},{8,10},{10,8},{12,14},{14,12},{16,18},{18,... | collective-permute-start | bytes 3145736 | tf_op jit(solution)/shard_map/ppermute | solution.py:129
  123.5 50.7 %collective-permute-start.6 = (f32[2048,128]{1,0:T(8,128)}, f32[2048,128]{1,0:T(8,128)S(1)}, u32[]{:S(2)}, u32[]{:S(2)}) collective-permute-start(f32[2048,128]{1,0:T(8,128)} %collective-permute-done.4.refs_0_), channel_id=1, source_target_pairs={{0,4},{2,6},{4,0},{6,2},{8,12},{10,14},{12,8},{14,10},{16,20},{18,... | collective-permute-start | bytes 3145736 | tf_op jit(solution)/shard_map/ppermute | solution.py:129
  125.1 50.6 %collective-permute-start.2 = (f32[16,136,128]{2,1,0:T(8,128)S(1)}, f32[16,136,128]{2,1,0:T(8,128)S(1)}, u32[]{:S(2)}, u32[]{:S(2)}) collective-permute-start(f32[16,136,128]{2,1,0:T(8,128)S(1)} %pad_maximum_fusion.1), channel_id=1, source_target_pairs={{0,8},{2,10},{4,12},{6,14},{8,0},{10,2},{12,4},{14,6},{16,24},{18,... | collective-permute-start | bytes 3342344 | tf_op jit(solution)/shard_map/ppermute | solution.py:129
  168.2 74.8 %collective-permute-start.21 = (f32[1024,128]{1,0:T(8,128)}, f32[1024,128]{1,0:T(8,128)}, u32[]{:S(2)}, u32[]{:S(2)}) collective-permute-start(f32[1024,128]{1,0:T(8,128)} %slice.155), channel_id=1, source_target_pairs={{0,4},{2,6},{4,0},{6,2},{8,12},{10,14},{12,8},{14,10},{16,20},{18,... | collective-permute-start | bytes 1572872 | tf_op jit(solution)/shard_map/ppermute | solution.py:129
  170.1 73.9 %collective-permute-start.22 = (f32[1024,128]{1,0:T(8,128)}, f32[1024,128]{1,0:T(8,128)}, u32[]{:S(2)}, u32[]{:S(2)}) collective-permute-start(f32[1024,128]{1,0:T(8,128)} %slice.156), channel_id=1, source_target_pairs={{0,2},{2,0},{4,6},{6,4},{8,10},{10,8},{12,14},{14,12},{16,18},{18,... | collective-permute-start | bytes 1572872 | tf_op jit(solution)/shard_map/ppermute | solution.py:129
  172.4 81.0 %collective-permute-start.17 = (f32[1024,128]{1,0:T(8,128)}, f32[1024,128]{1,0:T(8,128)}, u32[]{:S(2)}, u32[]{:S(2)}) collective-permute-start(f32[1024,128]{1,0:T(8,128)} %slice.153), channel_id=1, source_target_pairs={{0,4},{2,6},{4,0},{6,2},{8,12},{10,14},{12,8},{14,10},{16,20},{18,... | collective-permute-start | bytes 1572872 | tf_op jit(solution)/shard_map/ppermute | solution.py:129
  174.3 80.3 %collective-permute-start.18 = (f32[1024,128]{1,0:T(8,128)}, f32[1024,128]{1,0:T(8,128)}, u32[]{:S(2)}, u32[]{:S(2)}) collective-permute-start(f32[1024,128]{1,0:T(8,128)} %slice.154), channel_id=1, source_target_pairs={{0,2},{2,0},{4,6},{6,4},{8,10},{10,8},{12,14},{14,12},{16,18},{18,... | collective-permute-start | bytes 1572872 | tf_op jit(solution)/shard_map/ppermute | solution.py:129
  177.0 48.0 %collective-permute-start.3 = (f32[16,136,128]{2,1,0:T(8,128)}, f32[16,136,128]{2,1,0:T(8,128)}, u32[]{:S(2)}, u32[]{:S(2)}) collective-permute-start(f32[16,136,128]{2,1,0:T(8,128)} %pad_maximum_fusion.2), channel_id=1, source_target_pairs={{0,16},{2,18},{4,20},{6,22},{8,24},{10,26},{12,28},{14,30},{16,0},... | collective-permute-start | bytes 3342344 | tf_op jit(solution)/shard_map/ppermute | solution.py:129
  225.0 37.7 %collective-permute-start.12 = (f32[1024,128]{1,0:T(8,128)S(1)}, f32[1024,128]{1,0:T(8,128)S(1)}, u32[]{:S(2)}, u32[]{:S(2)}) collective-permute-start(f32[1024,128]{1,0:T(8,128)S(1)} %copy-done.23), channel_id=1, source_target_pairs={{0,4},{2,6},{4,0},{6,2},{8,12},{10,14},{12,8},{14,10},{16,20},{18,... | collective-permute-start | bytes 1572872 | tf_op jit(solution)/shard_map/ppermute | solution.py:129
  243.0 19.7 %collective-permute-start.13 = (f32[1024,128]{1,0:T(8,128)S(1)}, f32[1024,128]{1,0:T(8,128)S(1)}, u32[]{:S(2)}, u32[]{:S(2)}) collective-permute-start(f32[1024,128]{1,0:T(8,128)S(1)} %copy-done.25), channel_id=1, source_target_pairs={{0,2},{2,0},{4,6},{6,4},{8,10},{10,8},{12,14},{14,12},{16,18},{18,... | collective-permute-start | bytes 1572872 | tf_op jit(solution)/shard_map/ppermute | solution.py:129
  244.0 26.4 %collective-permute-start.7 = (f32[1024,128]{1,0:T(8,128)S(1)}, f32[1024,128]{1,0:T(8,128)S(1)}, u32[]{:S(2)}, u32[]{:S(2)}) collective-permute-start(f32[1024,128]{1,0:T(8,128)S(1)} %copy-done.24), channel_id=1, source_target_pairs={{0,4},{2,6},{4,0},{6,2},{8,12},{10,14},{12,8},{14,10},{16,20},{18,... | collective-permute-start | bytes 1572872 | tf_op jit(solution)/shard_map/ppermute | solution.py:129
  253.4 16.9 %collective-permute-start.8 = (f32[1024,128]{1,0:T(8,128)S(1)}, f32[1024,128]{1,0:T(8,128)S(1)}, u32[]{:S(2)}, u32[]{:S(2)}) collective-permute-start(f32[1024,128]{1,0:T(8,128)S(1)} %copy-done.26), channel_id=1, source_target_pairs={{0,2},{2,0},{4,6},{6,4},{8,10},{10,8},{12,14},{14,12},{16,18},{18,... | collective-permute-start | bytes 1572872 | tf_op jit(solution)/shard_map/ppermute | solution.py:129
  281.2 4.4 %collective-permute-start.23 = (f32[512,1024]{1,0:T(8,128)}, f32[512,1024]{1,0:T(8,128)S(1)}, u32[]{:S(2)}, u32[]{:S(2)}) collective-permute-start(f32[512,1024]{1,0:T(8,128)} %constant_dynamic-slice_fusion), channel_id=1, source_target_pairs={{0,1},{1,0},{2,3},{3,2},{4,5},{5,4},{6,7},{7,6},{8,9},{9,8},{10,11... | collective-permute-start | bytes 6291464 | tf_op jit(solution)/shard_map/ppermute | solution.py:315
  (30 other events, 367.9 us)
